TPU v7x, 32 devices: a whole 2x2x4 slice. The times are simulated.
32 devices in a mesh: slides: 2 (over y), rows: 8 (over z, x), cols: 2 (over core).
Axes of the slice: x: 2, y: 2, z: 4, core: 2. Of those that a mesh axis runs over, the one named last changes fastest.
Arguments:
- tokens: bfloat16 [512, 32, 512], P(('slides', 'cols'), 'rows'), parts along dimension 0, may hold values from -6 to 6
- norm_gain: float32 [512], replicated, may hold values from 0.5 to 1.5
- w_in: bfloat16 [512, 2048], replicated, may hold values from -0.25 to 0.25
- w_bc: bfloat16 [512, 64], replicated, may hold values from -0.046875 to 0.046875
- rate_row: float32 [16, 1024], replicated, may hold values from 0.002 to 0.08
- rate_col: float32 [16, 1024], replicated, may hold values from 0.002 to 0.08
- skip_gain: float32 [1024], replicated, may hold values from 0.5 to 1.5
- w_out: bfloat16 [1024, 512], replicated, may hold values from -0.1875 to 0.1875
Outputs:
- mixed: bfloat16 [512, 32, 512], P(('slides', 'cols'), 'rows'), parts along dimension 0
There are 2 independent parts, one for each index of `slides`. A program takes and returns all parts, laid end to end along the dimension named above; an argument that names none is the same for every part. Nothing has to cross between parts.
All inputs are finite; a program needn't handle non-finite values.
Results may differ from a plain program's by a relative error of at most 0.013.
Values may be sent and summed in bfloat16 or wider, within the bound.
A program may use at most 64 MiB of HBM per device.

v0:
```python
import jax
import jax.numpy as jnp
from jax import lax
from jax.sharding import PartitionSpec as P


def prefix(shard, axis, combine, identity):
    size, here = (lax.axis_size(axis), lax.axis_index(axis))
    everything = jax.tree.map(
        lambda part, kind: lax.all_gather(part.astype(kind), axis),
        shard,
        (jnp.bfloat16, jnp.bfloat16),
    )
    start = jax.tree.map(
        lambda part, zero: jnp.broadcast_to(jnp.asarray(zero, part.dtype), part.shape),
        shard,
        identity,
    )

    def turn(k, before):
        reached = k < here
        new = combine(
            before, jax.tree.map(lambda part, own: part[k].astype(own.dtype), everything, shard)
        )
        return jax.tree.map(lambda a, b: jnp.where(reached, a, b), new, before)

    return lax.fori_loop(0, size, turn, start)


def block_scan(series, inject, readout, decay_factor, skip_weight, scan_axis):
    block_len = 16
    other_axis = 1 - scan_axis
    item_count = series.shape[other_axis]
    start_state = jnp.zeros((item_count, decay_factor.shape[0], decay_factor.shape[1]), jnp.float32)
    start_out = jnp.zeros(series.shape, jnp.float32)

    def one_block(block_id, carry):
        carried, outputs = carry
        first_row = block_id * block_len
        series_part = lax.dynamic_slice_in_dim(series, first_row, block_len, scan_axis).astype(
            jnp.float32
        )
        inject_part = lax.dynamic_slice_in_dim(inject, first_row, block_len, scan_axis).astype(
            jnp.float32
        )
        readout_part = lax.dynamic_slice_in_dim(readout, first_row, block_len, scan_axis).astype(
            jnp.float32
        )
        results = []
        for offset in range(block_len):
            value_now = lax.index_in_dim(series_part, offset, scan_axis, keepdims=False)
            inject_now = lax.index_in_dim(inject_part, offset, scan_axis, keepdims=False)
            read_now = lax.index_in_dim(readout_part, offset, scan_axis, keepdims=False)
            carried = decay_factor[None] * carried + inject_now[:, :, None] * value_now[:, None, :]
            results.append(
                jnp.einsum("ine,in->ie", carried, read_now, precision=lax.Precision.HIGHEST)
                + skip_weight * value_now
            )
        stacked = jnp.stack(results, axis=scan_axis)
        outputs = lax.dynamic_update_slice_in_dim(outputs, stacked, first_row, scan_axis)
        return (carried, outputs)

    carried, outputs = lax.fori_loop(
        0, series.shape[scan_axis] // block_len, one_block, (start_state, start_out)
    )
    return (outputs, carried)


def chain_join(earlier, later):
    return (earlier[0] * later[0], later[0][None] * earlier[1] + later[1])


def per_device(tokens, norm_gain, w_in, w_bc, rate_row, rate_col, skip_gain, w_out):
    inner_width = w_out.shape[0]
    state_width = rate_row.shape[0]
    as_float = tokens.astype(jnp.float32)
    scale_now = lax.rsqrt(jnp.mean(as_float * as_float, axis=-1, keepdims=True) + 1e-05)
    normed = (as_float * scale_now * norm_gain).astype(jnp.bfloat16)
    project = jnp.dot(normed, w_in, preferred_element_type=jnp.float32)
    inputs_u = project[..., :inner_width].astype(jnp.bfloat16)
    gate_z = project[..., inner_width:].astype(jnp.bfloat16)
    mixers = jnp.dot(normed, w_bc, preferred_element_type=jnp.float32).astype(jnp.bfloat16)
    col_vectors = mixers[..., 2 * state_width :]
    moved_u, moved_vectors = (
        lax.all_to_all(inputs_u, "rows", split_axis=0, concat_axis=1, tiled=True),
        lax.all_to_all(
            mixers[..., : 2 * state_width], "rows", split_axis=0, concat_axis=1, tiled=True
        ),
    )
    row_out, _ = block_scan(
        moved_u,
        moved_vectors[..., :state_width],
        moved_vectors[..., state_width:],
        jnp.exp(-rate_row),
        skip_gain,
        1,
    )
    row_mixed = row_out.astype(jnp.bfloat16)
    back_home = lax.all_to_all(row_mixed, "rows", split_axis=1, concat_axis=0, tiled=True)
    col_readout = col_vectors[..., state_width:]
    col_out, end_state = block_scan(
        back_home, col_vectors[..., :state_width], col_readout, jnp.exp(-rate_col), 1.0, 0
    )
    height = back_home.shape[0]
    total_decay = jnp.exp(-rate_col * height)
    incoming = prefix(
        (total_decay, end_state),
        "cols",
        chain_join,
        (jnp.ones_like(total_decay), jnp.zeros_like(end_state)),
    )[1]

    def correct(block_id, outputs):
        first_row = block_id * 16
        read_part = lax.dynamic_slice_in_dim(col_readout, first_row, 16, 0).astype(jnp.float32)
        steps_ahead = (first_row + 1 + jnp.arange(16, dtype=jnp.int32)).astype(jnp.float32)
        powers = jnp.exp(-rate_col[None] * steps_ahead[:, None, None])
        carried_part = jnp.einsum(
            "lwn,lne,wne->lwe", read_part, powers, incoming, precision=lax.Precision.HIGHEST
        )
        updated = lax.dynamic_slice_in_dim(outputs, first_row, 16, 0) + carried_part
        return lax.dynamic_update_slice_in_dim(outputs, updated, first_row, 0)

    col_out = lax.fori_loop(0, height // 16, correct, col_out)
    gated = (col_out * jax.nn.silu(gate_z.astype(jnp.float32))).astype(jnp.bfloat16)
    return jnp.dot(gated, w_out, preferred_element_type=jnp.float32).astype(jnp.bfloat16)


def solution(mesh):
    placed = (P(("slides", "cols"), "rows", None), P(), P(), P(), P(), P(), P(), P())
    return jax.shard_map(
        per_device,
        mesh=mesh,
        in_specs=placed,
        out_specs=P(("slides", "cols"), "rows", None),
        check_vma=False,
    )
```

profile of v0, /device:TPU:0, one launch (start us, length us, event | category | flops | bytes accessed | tf_op | source)
XLA Modules:
  0.0 232.9 jit_solution(4700963122558836914)
XLA Ops:
  5.0 7.3 %all-to-all-start = ((bf16[8,2,1024]{2,1,0:T(2,128)(2,1)}), bf16[8,2,1024]{2,1,0:T(2,128)(2,1)S(1)}, u32[]{:S(2)}, u32[]{:S(2)}) async-start(bf16[8,2,1024]{2,1,0:T(2,128)(2,1)} %reshape.149), calls=%async_computation | async-start | bytes 65536 | tf_op jit(solution)/shard_map/all_to_all | solution.py:86
  15.1 1.8 copy.78
  16.9 2.1 all-to-all-done
  19.0 3.8 %all-to-all-start.1 = ((bf16[128,4,1024]{2,1,0:T(4,128)(2,1)}), bf16[128,4,1024]{2,1,0:T(4,128)(2,1)S(1)}, u32[]{:S(2)}, u32[]{:S(2)}) async-start(bf16[128,4,1024]{2,1,0:T(4,128)(2,1)} %copy.78), calls=%async_computation.1 | async-start | bytes 2097152 | tf_op jit(solution)/shard_map/all_to_all | solution.py:85
  23.9 24.4 %all-to-all-done.1 = bf16[128,4,1024]{2,1,0:T(4,128)(2,1)S(1)} async-done(((bf16[128,4,1024]{2,1,0:T(4,128)(2,1)}), bf16[128,4,1024]{2,1,0:T(4,128)(2,1)S(1)}, u32[]{:S(2)}, u32[]{:S(2)}) %all-to-all-start.1) | async-done | bytes 1048608 | tf_op jit(solution)/shard_map/all_to_all | solution.py:85
  50.7 44.3 %while.62 = (s32[]{:T(128)}, f32[16,16,1024]{2,1,0:T(8,128)}, bf16[16,32,1024]{2,0,1:T(8,128)(2,1)}, f32[16,1024]{1,0:T(8,128)S(1)}, bf16[16,32,16]{2,0,1:T(8,12...) while((s32[]{:T(128)}, f32[16,16,1024]{2,1,0:T(8,128)}, ...), condition=%wide.region_2.0_spmd.clone, body=%wide.region_1.0_spmd.clone.sunk | while | flops 94638096 | bytes 42889080 | solution.py:63
  61.7 2.3 multiply_add_fusion.115
  75.6 2.0 fusion.297
  77.7 2.0 fusion.298
  84.4 2.3 multiply_add_fusion.115
  95.1 4.4 %all-to-all-start.2 = ((bf16[16,32,1024]{2,0,1:T(8,128)(2,1)}), bf16[16,32,1024]{2,0,1:T(8,128)(2,1)}, u32[]{:S(2)}, u32[]{:S(2)}) async-start(bf16[16,32,1024]{2,0,1:T(8,128)(2,1)} %get-tuple-element.491), calls=%async_computation.2 | async-start | bytes 2097152 | tf_op jit(solution)/shard_map/all_to_all | solution.py:99
  99.7 1.9 all-gather
  101.5 23.3 %all-to-all-done.2 = bf16[16,32,1024]{2,0,1:T(8,128)(2,1)} async-done(((bf16[16,32,1024]{2,0,1:T(8,128)(2,1)}), bf16[16,32,1024]{2,0,1:T(8,128)(2,1)}, u32[]{:S(2)}, u32[]{:S(2)}) %all-to-all-start.2) | async-done | bytes 1048608 | tf_op jit(solution)/shard_map/all_to_all | solution.py:99
  124.8 3.0 %copy.80 = bf16[16,8,4,1024]{3,2,0,1:T(4,128)(2,1)} copy(bf16[16,8,4,1024]{3,0,2,1:T(8,128)(2,1)} %bitcast.13) | data formatting | bytes 2097152 | tf_op jit(solution)/shard_map/all_to_all | solution.py:99
  127.9 1.8 broadcast_in_dim.18
  129.7 69.7 %while.63 = (s32[]{:T(128)}, f32[4,16,1024]{2,1,0:T(8,128)S(1)}, f32[128,4,1024]{2,1,0:T(4,128)}, f32[16,1024]{1,0:T(8,128)S(1)}, bf16[128,4,16]{0,2,1:T(8,128)(...) while((s32[]{:T(128)}, f32[4,16,1024]{2,1,0:T(8,128)S(1)}, ...), condition=%wide.region_4.0_spmd.clone, body=%wide.region_3.0_spmd.clone.sunk | while | flops 27526164 | bytes 9698083 | solution.py:63
  199.5 2.0 all-gather.1
  201.8 26.2 %while.61 = (s32[]{:T(128)}, f32[128,4,1024]{2,1,0:T(4,128)}, f32[1,16,1024]{2,1,0:T(8,128)S(1)}, bf16[128,4,16]{2,1,0:T(4,128)(2,1)S(1)}, f32[4,16,1024]{2,1,0:...) while((s32[]{:T(128)}, f32[128,4,1024]{2,1,0:T(4,128)}, f32[1,16,1024]{2,1,0:T(8,128)S(1)}, ...), condition=%wide.region_8.9_spmd, body=%wide.region_7.8_spmd.sunk | while | flops 3408935 | bytes 3483939 | solution.py:124
  203.4 1.7 fusion.275
  206.7 1.8 fusion.275
  210.0 1.7 fusion.275
  213.2 1.7 fusion.275
  216.5 1.8 fusion.275
  228.0 3.7 %convolution_convert_fusion.1 = bf16[128,4,512]{2,0,1:T(8,128)(2,1)S(1)} fusion(bf16[1024,512]{1,0:T(8,128)(2,1)} %param.23, f32[128,4,1024]{2,1,0:T(4,128)} %get-tuple-element.495, bf16[128,4,2048]{2,0,1:T(8,128)(2,1)} %copy-done.5), kind=kOutput, calls=%fused_computation.390 | convolution fusion | flops 540803072 | bytes 4718592 | tf_op jit(solution)/shard_map/dot_general | solution.py:126
  (528 shorter events, 133.1 us)
Async XLA Ops:
  0.0 12.3 %copy-start = (bf16[512,2048]{1,0:T(8,128)(2,1)S(1)}, bf16[512,2048]{1,0:T(8,128)(2,1)}, u32[]{:S(2)}) copy-start(bf16[512,2048]{1,0:T(8,128)(2,1)} %param.18) | copy-start | bytes 6291460
  5.0 14.0 %all-to-all-start = ((bf16[8,2,1024]{2,1,0:T(2,128)(2,1)}), bf16[8,2,1024]{2,1,0:T(2,128)(2,1)S(1)}, u32[]{:S(2)}, u32[]{:S(2)}) async-start(bf16[8,2,1024]{2,1,0:T(2,128)(2,1)} %reshape.149), calls=%async_computation | async-start | bytes 65536 | tf_op jit(solution)/shard_map/all_to_all | solution.py:86
  13.6 1.4 copy-start.5
  15.1 7.8 %copy-start.16 = (f32[16,1024]{1,0:T(8,128)S(1)}, f32[16,1024]{1,0:T(8,128)}, u32[]{:S(2)}) copy-start(f32[16,1024]{1,0:T(8,128)} %param.20) | copy-start | bytes 196612
  19.0 29.3 %all-to-all-start.1 = ((bf16[128,4,1024]{2,1,0:T(4,128)(2,1)}), bf16[128,4,1024]{2,1,0:T(4,128)(2,1)S(1)}, u32[]{:S(2)}, u32[]{:S(2)}) async-start(bf16[128,4,1024]{2,1,0:T(4,128)(2,1)} %copy.78), calls=%async_computation.1 | async-start | bytes 2097152 | tf_op jit(solution)/shard_map/all_to_all | solution.py:85
  23.0 27.7 %copy-start.3 = (f32[1024]{0:T(1024)S(1)}, f32[1024]{0:T(1024)}, u32[]{:S(2)}) copy-start(f32[1024]{0:T(1024)} %param.22) | copy-start | bytes 12292
  54.1 3.0 %copy-start.1 = (f32[16,16,1024]{2,1,0:T(8,128)S(1)}, f32[16,16,1024]{2,1,0:T(8,128)}, u32[]{:S(2)}) copy-start(f32[16,16,1024]{2,1,0:T(8,128)} %get-tuple-element.1202) | copy-start | bytes 3145732 | tf_op jit(solution)/shard_map/while
  54.1 3.0 %copy-start.4 = (f32[16,16]{1,0:T(8,128)S(1)}, f32[16,16]{1,0:T(8,128)}, u32[]{:S(2)}) copy-start(f32[16,16]{1,0:T(8,128)} %get-tuple-element.1055) | copy-start | bytes 3076 | tf_op jit(solution)/shard_map/while
  54.1 3.0 %copy-start.14 = (bf16[16,16,1]{1,0,2:T(8,128)(2,1)S(1)}, bf16[16,16,1]{1,0,2:T(8,128)(2,1)}, u32[]{:S(2)}) copy-start(bf16[16,16,1]{1,0,2:T(8,128)(2,1)} %get-tuple-element.1058) | copy-start | bytes 1540 | tf_op jit(solution)/shard_map/while
  59.1 1.2 copy-start.11
  61.7 2.3 copy-start.10
  64.0 7.0 %copy-start.2 = (f32[16,16,1024]{2,1,0:T(8,128)}, f32[16,16,1024]{2,1,0:T(8,128)S(1)}, u32[]{:S(2)}) copy-start(f32[16,16,1024]{2,1,0:T(8,128)S(1)} %get-tuple-element.1229) | copy-start | bytes 3145732 | tf_op jit(solution)/shard_map/while
  65.9 1.5 copy-start.7
  66.7 1.6 copy-start.6
  75.6 4.1 %copy-start.1 = (f32[16,16,1024]{2,1,0:T(8,128)S(1)}, f32[16,16,1024]{2,1,0:T(8,128)}, u32[]{:S(2)}) copy-start(f32[16,16,1024]{2,1,0:T(8,128)} %get-tuple-element.1202) | copy-start | bytes 3145732 | tf_op jit(solution)/shard_map/while
  75.6 4.1 %copy-start.4 = (f32[16,16]{1,0:T(8,128)S(1)}, f32[16,16]{1,0:T(8,128)}, u32[]{:S(2)}) copy-start(f32[16,16]{1,0:T(8,128)} %get-tuple-element.1055) | copy-start | bytes 3076 | tf_op jit(solution)/shard_map/while
  75.6 4.1 %copy-start.14 = (bf16[16,16,1]{1,0,2:T(8,128)(2,1)S(1)}, bf16[16,16,1]{1,0,2:T(8,128)(2,1)}, u32[]{:S(2)}) copy-start(bf16[16,16,1]{1,0,2:T(8,128)(2,1)} %get-tuple-element.1058) | copy-start | bytes 1540 | tf_op jit(solution)/shard_map/while
  84.3 2.3 copy-start.10
  86.7 7.0 %copy-start.2 = (f32[16,16,1024]{2,1,0:T(8,128)}, f32[16,16,1024]{2,1,0:T(8,128)S(1)}, u32[]{:S(2)}) copy-start(f32[16,16,1024]{2,1,0:T(8,128)S(1)} %get-tuple-element.1229) | copy-start | bytes 3145732 | tf_op jit(solution)/shard_map/while
  88.6 1.5 copy-start.7
  89.4 1.6 copy-start.6
  95.0 4.4 %copy-start.18 = (bf16[128,4,64]{0,2,1:T(8,128)(2,1)S(1)}, bf16[128,4,64]{0,2,1:T(8,128)(2,1)}, u32[]{:S(2)}) copy-start(bf16[128,4,64]{0,2,1:T(8,128)(2,1)} %copy-done.17) | copy-start | bytes 196612
  95.0 4.6 %copy-start.15 = (f32[16,1024]{1,0:T(8,128)S(1)}, f32[16,1024]{1,0:T(8,128)}, u32[]{:S(2)}) copy-start(f32[16,1024]{1,0:T(8,128)} %param.21) | copy-start | bytes 196612
  95.1 29.8 %all-to-all-start.2 = ((bf16[16,32,1024]{2,0,1:T(8,128)(2,1)}), bf16[16,32,1024]{2,0,1:T(8,128)(2,1)}, u32[]{:S(2)}, u32[]{:S(2)}) async-start(bf16[16,32,1024]{2,0,1:T(8,128)(2,1)} %get-tuple-element.491), calls=%async_computation.2 | async-start | bytes 2097152 | tf_op jit(solution)/shard_map/all_to_all | solution.py:99
  (10 other events, 10.3 us)
where the time goes:
time: 234 us; the launch traced here: 233 us
  matrix products  81.9 us (35%)
  other arithmetic  51.2 us (22%)
  waiting for transfers between devices  49.9 us (21%)
  local copies, waits for them, and re-layouts  27.4 us (12%)
  starting transfers between devices  15.5 us (7%)
  blocking collectives  3.85 us (2%)
  loops' own time  3.01 us (1%)
    dot_general x160, matrix products, one_block(): jnp.einsum('ine,in->ie', carried, read_now, precision=lax.Precision.HIGHEST)  75.8 us
    all_to_all x1, waiting for transfers between devices, per_device(): lax.all_to_all(inputs_u, 'rows', split_axis=0, concat_axis=1, tiled=True)  24.4 us
    all_to_all x1, waiting for transfers between devices, per_device(): lax.all_to_all(row_mixed, 'rows', split_axis=1, concat_axis=0, tiled=True)  23.3 us
    dynamic_update_slice x8, other arithmetic, correct(): return lax.dynamic_update_slice_in_dim(outputs, updated, first_row, 0)  13.9 us
    dot_general x8, other arithmetic, correct(): jnp.einsum('lwn,lne,wne->lwe', read_part, powers, incoming, precision=lax...  10.4 us
    convert_element_type x10, other arithmetic, one_block(): lax.dynamic_slice_in_dim(series, first_row, block_len, scan_axis)  9.74 us
    add x10, other arithmetic, one_block(): decay_factor[None] * carried  9.09 us
    dynamic_update_slice x10, local copies, waits for them, and re-layouts, one_block(): lax.dynamic_update_slice_in_dim(outputs, stacked, first_row, scan_axis)  7.58 us
  transfers between devices with their start and end apart: 3, of which 3 were waited for; matrix products, arithmetic and copies ran while one was open for 2% of the time, Pallas kernels for 0%

commit v1 on v0

--- a/solution.py
+++ b/solution.py
@@ -2,6 +2,28 @@
 import jax.numpy as jnp
 from jax import lax
 from jax.sharding import PartitionSpec as P
+
+
+def split_up(x, dim, devices):
+    before, after = (x.shape[:dim], x.shape[dim + 1 :])
+    return jnp.moveaxis(x.reshape(*before, devices, -1, *after), dim, 0)
+
+
+def laid_out(blocks, dim):
+    lengths = list(blocks.shape[1:])
+    lengths[dim] *= blocks.shape[0]
+    return jnp.moveaxis(blocks, 0, dim).reshape(lengths)
+
+
+def swapped_with_each(x, axis, split_dim, concat_dim):
+    size, position = (lax.axis_size(axis), lax.axis_index(axis))
+    tiles = split_up(x, split_dim, size)
+    finished = [tiles[position]]
+    for step in range(1, size):
+        sent = tiles[position ^ step]
+        finished.append(lax.ppermute(sent, axis, [(i, i ^ step) for i in range(size)]))
+    tiles = jnp.stack(finished)[position ^ jnp.arange(size)]
+    return laid_out(tiles, concat_dim)
 
 
 def prefix(shard, axis, combine, identity):
@@ -82,7 +104,7 @@
     mixers = jnp.dot(normed, w_bc, preferred_element_type=jnp.float32).astype(jnp.bfloat16)
     col_vectors = mixers[..., 2 * state_width :]
     moved_u, moved_vectors = (
-        lax.all_to_all(inputs_u, "rows", split_axis=0, concat_axis=1, tiled=True),
+        swapped_with_each(inputs_u, "rows", 0, 1),
         lax.all_to_all(
             mixers[..., : 2 * state_width], "rows", split_axis=0, concat_axis=1, tiled=True
         ),

time: 234 us -> 226 us (0.966)
  waiting for transfers between devices: 49.9 us -> 30.1 us
  starting transfers between devices: 15.5 us -> 22.8 us
  local copies, waits for them, and re-layouts: 27.4 us -> 32 us
    all_to_all x1 -> x0, waiting for transfers between devices: 24.4 us -> none  [per_device(): lax.all_to_all(inputs_u, 'rows', split_axis=0, concat_axis=1, tiled=True)]
    ppermute x0 -> x7, starting transfers between devices: none -> 12.6 us  [swapped_with_each(): lax.ppermute(sent, axis, [(i, i ^ step) for i in range(size)])]
    unnamed x17 -> x29, local copies, waits for them, and re-layouts: 2.43 us -> 7.61 us
    all_to_all x1 -> x0, starting transfers between devices: 3.85 us -> none  [per_device(): lax.all_to_all(inputs_u, 'rows', split_axis=0, concat_axis=1, tiled=True)]
    all_to_all x1, waiting for transfers between devices: 2.15 us -> 5.79 us  [per_device(): lax.all_to_all(mixers[..., :2 * state_width], 'rows', split_axis=0, conca...]
    all_to_all x1, starting transfers between devices: 7.28 us -> 4.87 us  [per_device(): lax.all_to_all(mixers[..., :2 * state_width], 'rows', split_axis=0, conca...]
  transfers between devices with their start and end apart: 3 -> 9, of which waited for: 3 -> 3; matrix products, arithmetic and copies ran while one was open for 2% -> 3% of each run, Pallas kernels for 0% -> 0%
where the time goes in v1:
time: 226 us; the launch traced here: 225 us
  matrix products  81 us (36%)
  other arithmetic  52 us (23%)
  local copies, waits for them, and re-layouts  32 us (14%)
  waiting for transfers between devices  30.1 us (13%)
  starting transfers between devices  22.8 us (10%)
  blocking collectives  3.85 us (2%)
  loops' own time  3 us (1%)
    dot_general x160, matrix products, one_block(): jnp.einsum('ine,in->ie', carried, read_now, precision=lax.Precision.HIGHEST)  75.8 us
    all_to_all x1, waiting for transfers between devices, per_device(): lax.all_to_all(row_mixed, 'rows', split_axis=1, concat_axis=0, tiled=True)  22.2 us
    dynamic_update_slice x8, other arithmetic, correct(): return lax.dynamic_update_slice_in_dim(outputs, updated, first_row, 0)  13.8 us
    ppermute x7, starting transfers between devices, swapped_with_each(): lax.ppermute(sent, axis, [(i, i ^ step) for i in range(size)])  12.6 us
    dot_general x8, other arithmetic, correct(): jnp.einsum('lwn,lne,wne->lwe', read_part, powers, incoming, precision=lax...  10.4 us
    convert_element_type x10, other arithmetic, one_block(): lax.dynamic_slice_in_dim(series, first_row, block_len, scan_axis)  9.72 us
    add x10, other arithmetic, one_block(): decay_factor[None] * carried  9.09 us
    unnamed x29, local copies, waits for them, and re-layouts  7.61 us
  transfers between devices with their start and end apart: 9, of which 3 were waited for; matrix products, arithmetic and copies ran while one was open for 3% of the time, Pallas kernels for 0%

profile of v1, /device:TPU:0, one launch (start us, length us, event | category | flops | bytes accessed | tf_op | source)
XLA Modules:
  0.0 225.0 jit_solution(10001159427903383349)
XLA Ops:
  6.7 3.0 %collective-permute-start = (bf16[16,4,1024]{2,0,1:T(8,128)(2,1)}, bf16[16,4,1024]{2,0,1:T(8,128)(2,1)}, u32[]{:S(2)}, u32[]{:S(2)}) collective-permute-start(bf16[16,4,1024]{2,0,1:T(8,128)(2,1)} %get-tuple-element.797), channel_id=1, source_target_pairs={{0,2},{2,0},{4,6},{6,4},{8,10},{10,8},{12,14},{14,12},{1,3},{3,1},... | collective-permute-start | bytes 393224 | tf_op jit(solution)/shard_map/ppermute | solution.py:24
  11.3 3.0 %collective-permute-start.3 = (bf16[16,4,1024]{2,0,1:T(8,128)(2,1)}, bf16[16,4,1024]{2,0,1:T(8,128)(2,1)}, u32[]{:S(2)}, u32[]{:S(2)}) collective-permute-start(bf16[16,4,1024]{2,0,1:T(8,128)(2,1)} %get-tuple-element.794), channel_id=1, source_target_pairs={{0,8},{2,10},{4,12},{6,14},{8,0},{10,2},{12,4},{14,6},{1,9},{3,11}... | collective-permute-start | bytes 393224 | tf_op jit(solution)/shard_map/ppermute | solution.py:24
  17.4 4.9 %all-to-all-start = ((bf16[8,2,1024]{2,1,0:T(2,128)(2,1)}), bf16[8,2,1024]{2,1,0:T(2,128)(2,1)S(1)}, u32[]{:S(2)}, u32[]{:S(2)}) async-start(bf16[8,2,1024]{2,1,0:T(2,128)(2,1)} %reshape.181), calls=%async_computation | async-start | bytes 65536 | tf_op jit(solution)/shard_map/all_to_all | solution.py:108
  23.2 5.8 %all-to-all-done = bf16[8,2,1024]{2,1,0:T(2,128)(2,1)S(1)} async-done(((bf16[8,2,1024]{2,1,0:T(2,128)(2,1)}), bf16[8,2,1024]{2,1,0:T(2,128)(2,1)S(1)}, u32[]{:S(2)}, u32[]{:S(2)}) %all-to-all-start) | async-done | bytes 32800 | tf_op jit(solution)/shard_map/all_to_all | solution.py:108
  29.9 1.8 collective-permute-start.5
  32.7 2.0 collective-permute-start.6
  38.4 2.1 collective-permute-done.6
  43.2 44.3 %while.62 = (s32[]{:T(128)}, f32[16,16,1024]{2,1,0:T(8,128)}, bf16[16,32,1024]{2,0,1:T(8,128)(2,1)}, f32[16,1024]{1,0:T(8,128)S(1)}, bf16[16,32,16]{2,0,1:T(8,12...) while((s32[]{:T(128)}, f32[16,16,1024]{2,1,0:T(8,128)}, ...), condition=%wide.region_2.0_spmd.clone, body=%wide.region_1.0_spmd.clone.sunk | while | flops 94638096 | bytes 42889080 | solution.py:85
  54.2 2.3 %multiply_add_fusion.115 = (f32[16,16,1024]{2,1,0:T(8,128)S(1)}, f32[16,16,1024]{2,1,0:T(8,128)S(1)}, f32[16,16,1024]{2,1,0:T(8,128)S(1)}) fusion(f32[16,1024]{1,0:T(8,128)S(1)} %get-tuple-element.1081, f32[16,16]{1,0:T(8,128)S(1)} %get-tuple-element.1082, f32[16,1024]{1,0:T(8,128)S(1)} %get-tuple-element.1083, f32[16,16]{1,0:T(8,128)S(1)} %get-tuple-element.1084, ...), kind=kLoop, calls=%fused_computation.3.clone.1 | loop fusion | flops 12845056 | bytes 5324801 | tf_op jit(solution)/shard_map/while/body/eval_jaxpr/add | solution.py:76
  68.1 2.0 fusion.298
  70.2 2.0 fusion.299
  76.9 2.3 %multiply_add_fusion.115 = (f32[16,16,1024]{2,1,0:T(8,128)S(1)}, f32[16,16,1024]{2,1,0:T(8,128)S(1)}, f32[16,16,1024]{2,1,0:T(8,128)S(1)}) fusion(f32[16,1024]{1,0:T(8,128)S(1)} %get-tuple-element.1081, f32[16,16]{1,0:T(8,128)S(1)} %get-tuple-element.1082, f32[16,1024]{1,0:T(8,128)S(1)} %get-tuple-element.1083, f32[16,16]{1,0:T(8,128)S(1)} %get-tuple-element.1084, ...), kind=kLoop, calls=%fused_computation.3.clone.1 | loop fusion | flops 12845056 | bytes 5324801 | tf_op jit(solution)/shard_map/while/body/eval_jaxpr/add | solution.py:76
  87.5 5.3 %all-to-all-start.1 = ((bf16[16,32,1024]{2,0,1:T(8,128)(2,1)}), bf16[16,32,1024]{2,0,1:T(8,128)(2,1)}, u32[]{:S(2)}, u32[]{:S(2)}) async-start(bf16[16,32,1024]{2,0,1:T(8,128)(2,1)} %get-tuple-element.491), calls=%async_computation.1 | async-start | bytes 2097152 | tf_op jit(solution)/shard_map/all_to_all | solution.py:121
  93.0 1.9 all-gather
  94.9 22.2 %all-to-all-done.1 = bf16[16,32,1024]{2,0,1:T(8,128)(2,1)} async-done(((bf16[16,32,1024]{2,0,1:T(8,128)(2,1)}), bf16[16,32,1024]{2,0,1:T(8,128)(2,1)}, u32[]{:S(2)}, u32[]{:S(2)}) %all-to-all-start.1) | async-done | bytes 1048608 | tf_op jit(solution)/shard_map/all_to_all | solution.py:121
  117.1 3.0 %copy.70 = bf16[16,8,4,1024]{3,2,0,1:T(4,128)(2,1)} copy(bf16[16,8,4,1024]{3,0,2,1:T(8,128)(2,1)} %bitcast.28) | data formatting | bytes 2097152 | tf_op jit(solution)/shard_map/all_to_all | solution.py:121
  120.1 1.9 broadcast_in_dim.18
  122.0 69.7 %while.63 = (s32[]{:T(128)}, f32[4,16,1024]{2,1,0:T(8,128)S(1)}, f32[128,4,1024]{2,1,0:T(4,128)}, f32[16,1024]{1,0:T(8,128)S(1)}, bf16[128,4,16]{0,2,1:T(8,128)(...) while((s32[]{:T(128)}, f32[4,16,1024]{2,1,0:T(8,128)S(1)}, ...), condition=%wide.region_4.0_spmd.clone, body=%wide.region_3.0_spmd.clone.sunk | while | flops 27526164 | bytes 9698083 | solution.py:85
  191.7 2.0 all-gather.1
  194.0 26.1 %while.61 = (s32[]{:T(128)}, f32[128,4,1024]{2,1,0:T(4,128)}, f32[1,16,1024]{2,1,0:T(8,128)S(1)}, bf16[128,4,16]{2,1,0:T(4,128)(2,1)S(1)}, f32[4,16,1024]{2,1,0:...) while((s32[]{:T(128)}, f32[128,4,1024]{2,1,0:T(4,128)}, f32[1,16,1024]{2,1,0:T(8,128)S(1)}, ...), condition=%wide.region_8.9_spmd, body=%wide.region_7.8_spmd.sunk | while | flops 3408935 | bytes 3483939 | solution.py:146
  195.6 1.7 fusion.276
  215.1 1.7 fusion.276
  218.4 1.7 fusion.276
  220.1 3.7 %convolution_convert_fusion.1 = bf16[128,4,512]{2,0,1:T(8,128)(2,1)S(1)} fusion(bf16[1024,512]{1,0:T(8,128)(2,1)} %param.23, f32[128,4,1024]{2,1,0:T(4,128)} %get-tuple-element.495, bf16[128,4,2048]{2,0,1:T(8,128)(2,1)} %copy-done.6), kind=kOutput, calls=%fused_computation.391 | convolution fusion | flops 540803072 | bytes 4718592 | tf_op jit(solution)/shard_map/dot_general | solution.py:148
  (555 shorter events, 145.8 us)
Async XLA Ops:
  0.0 3.0 %copy-start = (bf16[512,2048]{1,0:T(8,128)(2,1)S(1)}, bf16[512,2048]{1,0:T(8,128)(2,1)}, u32[]{:S(2)}) copy-start(bf16[512,2048]{1,0:T(8,128)(2,1)} %param.18) | copy-start | bytes 6291460
  5.6 9.9 %copy-start.21 = (bf16[512,64]{0,1:T(8,128)(2,1)S(1)}, bf16[512,64]{0,1:T(8,128)(2,1)}, u32[]{:S(2)}) copy-start(bf16[512,64]{0,1:T(8,128)(2,1)} %param.19) | copy-start | bytes 196612
  5.7 9.8 %copy-start.8 = (bf16[128,4,512]{2,1,0:T(4,128)(2,1)S(1)}, bf16[128,4,512]{2,1,0:T(4,128)(2,1)}, u32[]{:S(2)}) copy-start(bf16[128,4,512]{2,1,0:T(4,128)(2,1)} %copy-done.7) | copy-start | bytes 1572868
  6.7 25.0 %copy-start.4 = (bf16[8,16,4,1024]{3,1,0,2:T(8,128)(2,1)S(1)}, bf16[8,16,4,1024]{3,1,0,2:T(8,128)(2,1)}, u32[]{:S(2)}) copy-start(bf16[8,16,4,1024]{3,1,0,2:T(8,128)(2,1)} %get-tuple-element.798) | copy-start | bytes 3145732
  6.7 23.2 %collective-permute-start = (bf16[16,4,1024]{2,0,1:T(8,128)(2,1)}, bf16[16,4,1024]{2,0,1:T(8,128)(2,1)}, u32[]{:S(2)}, u32[]{:S(2)}) collective-permute-start(bf16[16,4,1024]{2,0,1:T(8,128)(2,1)} %get-tuple-element.797), channel_id=1, source_target_pairs={{0,2},{2,0},{4,6},{6,4},{8,10},{10,8},{12,14},{14,12},{1,3},{3,1},... | collective-permute-start | bytes 393224 | tf_op jit(solution)/shard_map/ppermute | solution.py:24
  9.7 23.0 %collective-permute-start.1 = (bf16[16,4,1024]{2,0,1:T(8,128)(2,1)}, bf16[16,4,1024]{2,0,1:T(8,128)(2,1)}, u32[]{:S(2)}, u32[]{:S(2)}) collective-permute-start(bf16[16,4,1024]{2,0,1:T(8,128)(2,1)} %get-tuple-element.796), channel_id=1, source_target_pairs={{0,4},{2,6},{4,0},{6,2},{8,12},{10,14},{12,8},{14,10},{1,5},{3,7},... | collective-permute-start | bytes 393224 | tf_op jit(solution)/shard_map/ppermute | solution.py:24
  11.3 24.3 %collective-permute-start.2 = (bf16[16,4,1024]{2,0,1:T(8,128)(2,1)}, bf16[16,4,1024]{2,0,1:T(8,128)(2,1)}, u32[]{:S(2)}, u32[]{:S(2)}) collective-permute-start(bf16[16,4,1024]{2,0,1:T(8,128)(2,1)} %get-tuple-element.795), channel_id=1, source_target_pairs={{0,6},{2,4},{4,2},{6,0},{8,14},{10,12},{12,10},{14,8},{1,7},{3,5},... | collective-permute-start | bytes 393224 | tf_op jit(solution)/shard_map/ppermute | solution.py:24
  11.3 25.2 %collective-permute-start.3 = (bf16[16,4,1024]{2,0,1:T(8,128)(2,1)}, bf16[16,4,1024]{2,0,1:T(8,128)(2,1)}, u32[]{:S(2)}, u32[]{:S(2)}) collective-permute-start(bf16[16,4,1024]{2,0,1:T(8,128)(2,1)} %get-tuple-element.794), channel_id=1, source_target_pairs={{0,8},{2,10},{4,12},{6,14},{8,0},{10,2},{12,4},{14,6},{1,9},{3,11}... | collective-permute-start | bytes 393224 | tf_op jit(solution)/shard_map/ppermute | solution.py:24
  14.3 23.2 %collective-permute-start.4 = (bf16[16,4,1024]{2,0,1:T(8,128)(2,1)}, bf16[16,4,1024]{2,0,1:T(8,128)(2,1)}, u32[]{:S(2)}, u32[]{:S(2)}) collective-permute-start(bf16[16,4,1024]{2,0,1:T(8,128)(2,1)} %get-tuple-element.793), channel_id=1, source_target_pairs={{0,10},{2,8},{4,14},{6,12},{8,2},{10,0},{12,6},{14,4},{1,11},{3,9}... | collective-permute-start | bytes 393224 | tf_op jit(solution)/shard_map/ppermute | solution.py:24
  17.4 11.6 %all-to-all-start = ((bf16[8,2,1024]{2,1,0:T(2,128)(2,1)}), bf16[8,2,1024]{2,1,0:T(2,128)(2,1)S(1)}, u32[]{:S(2)}, u32[]{:S(2)}) async-start(bf16[8,2,1024]{2,1,0:T(2,128)(2,1)} %reshape.181), calls=%async_computation | async-start | bytes 65536 | tf_op jit(solution)/shard_map/all_to_all | solution.py:108
  29.9 8.4 %collective-permute-start.5 = (bf16[16,4,1024]{2,0,1:T(8,128)(2,1)}, bf16[16,4,1024]{2,0,1:T(8,128)(2,1)S(1)}, u32[]{:S(2)}, u32[]{:S(2)}) collective-permute-start(bf16[16,4,1024]{2,0,1:T(8,128)(2,1)} %get-tuple-element.792), channel_id=1, source_target_pairs={{0,12},{2,14},{4,8},{6,10},{8,4},{10,6},{12,0},{14,2},{1,13},{3,15... | collective-permute-start | bytes 393224 | tf_op jit(solution)/shard_map/ppermute | solution.py:24
  32.7 7.8 %collective-permute-start.6 = (bf16[16,4,1024]{2,0,1:T(8,128)(2,1)S(1)}, bf16[16,4,1024]{2,0,1:T(8,128)(2,1)S(1)}, u32[]{:S(2)}, u32[]{:S(2)}) collective-permute-start(bf16[16,4,1024]{2,0,1:T(8,128)(2,1)S(1)} %get-tuple-element.791), channel_id=1, source_target_pairs={{0,14},{2,12},{4,10},{6,8},{8,6},{10,4},{12,2},{14,0},{1,15},{3,13... | collective-permute-start | bytes 393224 | tf_op jit(solution)/shard_map/ppermute | solution.py:24
  36.5 6.7 %copy-start.3 = (f32[1024]{0:T(1024)S(1)}, f32[1024]{0:T(1024)}, u32[]{:S(2)}) copy-start(f32[1024]{0:T(1024)} %param.22) | copy-start | bytes 12292
  46.5 3.0 %copy-start.1 = (f32[16,16,1024]{2,1,0:T(8,128)S(1)}, f32[16,16,1024]{2,1,0:T(8,128)}, u32[]{:S(2)}) copy-start(f32[16,16,1024]{2,1,0:T(8,128)} %get-tuple-element.1210) | copy-start | bytes 3145732 | tf_op jit(solution)/shard_map/while
  46.5 3.0 %copy-start.5 = (f32[16,16]{1,0:T(8,128)S(1)}, f32[16,16]{1,0:T(8,128)}, u32[]{:S(2)}) copy-start(f32[16,16]{1,0:T(8,128)} %get-tuple-element.1063) | copy-start | bytes 3076 | tf_op jit(solution)/shard_map/while
  46.5 3.0 %copy-start.17 = (bf16[16,16,1]{1,0,2:T(8,128)(2,1)S(1)}, bf16[16,16,1]{1,0,2:T(8,128)(2,1)}, u32[]{:S(2)}) copy-start(bf16[16,16,1]{1,0,2:T(8,128)(2,1)} %get-tuple-element.1066) | copy-start | bytes 1540 | tf_op jit(solution)/shard_map/while
  56.5 7.0 %copy-start.2 = (f32[16,16,1024]{2,1,0:T(8,128)}, f32[16,16,1024]{2,1,0:T(8,128)S(1)}, u32[]{:S(2)}) copy-start(f32[16,16,1024]{2,1,0:T(8,128)S(1)} %get-tuple-element.1237) | copy-start | bytes 3145732 | tf_op jit(solution)/shard_map/while
  68.1 4.1 %copy-start.1 = (f32[16,16,1024]{2,1,0:T(8,128)S(1)}, f32[16,16,1024]{2,1,0:T(8,128)}, u32[]{:S(2)}) copy-start(f32[16,16,1024]{2,1,0:T(8,128)} %get-tuple-element.1210) | copy-start | bytes 3145732 | tf_op jit(solution)/shard_map/while
  68.1 4.1 %copy-start.5 = (f32[16,16]{1,0:T(8,128)S(1)}, f32[16,16]{1,0:T(8,128)}, u32[]{:S(2)}) copy-start(f32[16,16]{1,0:T(8,128)} %get-tuple-element.1063) | copy-start | bytes 3076 | tf_op jit(solution)/shard_map/while
  68.1 4.1 %copy-start.17 = (bf16[16,16,1]{1,0,2:T(8,128)(2,1)S(1)}, bf16[16,16,1]{1,0,2:T(8,128)(2,1)}, u32[]{:S(2)}) copy-start(bf16[16,16,1]{1,0,2:T(8,128)(2,1)} %get-tuple-element.1066) | copy-start | bytes 1540 | tf_op jit(solution)/shard_map/while
  79.2 7.0 %copy-start.2 = (f32[16,16,1024]{2,1,0:T(8,128)}, f32[16,16,1024]{2,1,0:T(8,128)S(1)}, u32[]{:S(2)}) copy-start(f32[16,16,1024]{2,1,0:T(8,128)S(1)} %get-tuple-element.1237) | copy-start | bytes 3145732 | tf_op jit(solution)/shard_map/while
  87.5 5.3 %copy-start.20 = (bf16[128,4,64]{0,2,1:T(8,128)(2,1)S(1)}, bf16[128,4,64]{0,2,1:T(8,128)(2,1)}, u32[]{:S(2)}) copy-start(bf16[128,4,64]{0,2,1:T(8,128)(2,1)} %copy-done.19) | copy-start | bytes 196612
  87.5 5.5 %copy-start.18 = (f32[16,1024]{1,0:T(8,128)S(1)}, f32[16,1024]{1,0:T(8,128)}, u32[]{:S(2)}) copy-start(f32[16,1024]{1,0:T(8,128)} %param.21) | copy-start | bytes 196612
  87.5 29.5 %all-to-all-start.1 = ((bf16[16,32,1024]{2,0,1:T(8,128)(2,1)}), bf16[16,32,1024]{2,0,1:T(8,128)(2,1)}, u32[]{:S(2)}, u32[]{:S(2)}) async-start(bf16[16,32,1024]{2,0,1:T(8,128)(2,1)} %get-tuple-element.491), calls=%async_computation.1 | async-start | bytes 2097152 | tf_op jit(solution)/shard_map/all_to_all | solution.py:121
  (19 other events, 24.5 us)
